TPU v7x, 32 devices: a whole 2x2x4 slice. The times are simulated.
32 devices in a mesh: row: 4 (over z), col: 4 (over y, x), agent: 2 (over core).
Axes of the slice: x: 2, y: 2, z: 4, core: 2. Of those that a mesh axis runs over, the one named last changes fastest.
Arguments:
- raster: bfloat16 [2, 512, 512, 128], P(None, 'row', ('col', 'agent')), may hold values from -6 to 6
- first_kernel: bfloat16 [3, 3, 128, 128], replicated, may hold values from -0.1875 to 0.1875
- first_bias: float32 [128], replicated, may hold values from -3 to 3
- second_kernel: bfloat16 [3, 3, 128, 128], replicated, may hold values from -0.1875 to 0.1875
- second_bias: float32 [128], replicated, may hold values from -3 to 3
- queries: bfloat16 [256, 128], P('agent'), may hold values from -64 to 64
- agent_slot: int32 [256], replicated, may hold values from 0 to 255, each once
- regions: int32 [256, 4], replicated, may hold values from 0 to 8, as said below
Outputs:
- log_heatmap: float32 [2, 512, 512, 256], P(None, 'row', ('col', 'agent'))
Inputs may be any that keep to these rules, and one draw needn't show every extreme that they name: regions[a,0] < regions[a,1] <= 8 and regions[a,2] < regions[a,3] <= 8.
All inputs are finite; a program needn't handle non-finite values.
Results may differ from a plain program's by a relative error of at most 0.0024.
Values may be sent and summed in bfloat16 or wider, within the bound.
A program may use at most 192 MiB of HBM per device.

v0:
```python
import jax
import jax.numpy as jnp
from jax import lax
from jax.sharding import PartitionSpec as P

BLOCK = 64


def padded_2(block, sides, width):
    for axis, dim in sides:
        count = lax.axis_size(axis)
        forward = [(i, i + 1) for i in range(count - 1)]
        backward = [(target, source) for source, target in forward]
        low = lax.ppermute(
            lax.slice_in_dim(block, block.shape[dim] - width, None, axis=dim), axis, forward
        )
        high = lax.ppermute(lax.slice_in_dim(block, 0, width, axis=dim), axis, backward)
        block = jnp.concatenate([low, block, high], axis=dim)
    return block


def dilated(padded, kernel, bias, dilation, out_rows, out_cols):
    scenes = padded.shape[0]
    channels = padded.shape[3]
    running = jnp.zeros((scenes * out_rows * out_cols, kernel.shape[3]), jnp.float32)
    for row_tap in range(3):
        for col_tap in range(3):
            tap_piece = padded[
                :,
                row_tap * dilation : row_tap * dilation + out_rows,
                col_tap * dilation : col_tap * dilation + out_cols,
                :,
            ]
            running = running + jnp.dot(
                tap_piece.reshape(-1, channels),
                kernel[row_tap, col_tap],
                preferred_element_type=jnp.float32,
            )
    result = jnp.maximum(running + bias, 0.0).astype(jnp.bfloat16)
    return result.reshape(scenes, out_rows, out_cols, -1)


def shards(
    raster, first_kernel, first_bias, second_kernel, second_bias, queries, agent_slot, regions
):
    scenes, tile_rows, tile_cols, channels = raster.shape
    row_start = lax.axis_index("row") * tile_rows
    col_start = lax.axis_index(("col", "agent")) * tile_cols
    near_field = padded_2(raster, (("row", 1), (("col", "agent"), 2)), 4)
    layer_one = dilated(near_field, first_kernel, first_bias, 4, tile_rows, tile_cols)
    far_field = padded_2(layer_one, (("row", 1), (("col", "agent"), 2)), 8)
    layer_two = dilated(far_field, second_kernel, second_bias, 8, tile_rows, tile_cols)
    everyone = lax.all_gather(queries, "agent", axis=0, tiled=True)
    ordered = jnp.take(everyone, agent_slot, axis=0)
    agents = ordered.shape[0]
    flat = layer_two.reshape(scenes, tile_rows * tile_cols, channels)
    logits = jnp.einsum("snc,ac->sna", flat, ordered, preferred_element_type=jnp.float32)
    block_rows = (row_start + jnp.arange(tile_rows, dtype=jnp.int32)) // BLOCK
    block_cols = (col_start + jnp.arange(tile_cols, dtype=jnp.int32)) // BLOCK
    row_ok = (block_rows[:, None] >= regions[None, :, 0]) & (
        block_rows[:, None] < regions[None, :, 1]
    )
    col_ok = (block_cols[:, None] >= regions[None, :, 2]) & (
        block_cols[:, None] < regions[None, :, 3]
    )
    valid = (row_ok[:, None, :] & col_ok[None, :, :]).reshape(1, tile_rows * tile_cols, agents)
    local_peak = jnp.max(jnp.where(valid, logits, -1e30), axis=1)
    peak = lax.pmax(local_peak, ("row", "col", "agent"))
    local_mass = jnp.sum(jnp.where(valid, jnp.exp(logits - peak[:, None, :]), 0.0), axis=1)
    mass = lax.psum(local_mass, ("row", "col", "agent"))
    normaliser = peak + jnp.log(mass)
    return (logits - normaliser[:, None, :]).reshape(scenes, tile_rows, tile_cols, agents)


def solution(mesh):
    in_specs = (
        P(None, "row", ("col", "agent"), None),
        P(),
        P(),
        P(),
        P(),
        P("agent", None),
        P(),
        P(),
    )
    out_specs = P(None, "row", ("col", "agent"), None)
    return jax.shard_map(shards, mesh=mesh, in_specs=in_specs, out_specs=out_specs, check_vma=False)
```

profile of v0, /device:TPU:0, one launch (start us, length us, event | category | flops | bytes accessed | tf_op | source)
XLA Modules:
  0.0 271.3 jit_solution(7832234871713748013)
XLA Ops:
  2.3 5.6 %collective-permute-start = (bf16[2,4,64,128]{3,2,1,0:T(8,128)(2,1)S(1)}, bf16[2,4,64,128]{3,2,1,0:T(8,128)(2,1)S(1)}, u32[]{:S(2)}, u32[]{:S(2)}) collective-permute-start(bf16[2,4,64,128]{3,2,1,0:T(8,128)(2,1)S(1)} %get-tuple-element.34), channel_id=1, source_target_pairs={{0,8},{8,16},{16,24},{1,9},{9,17},{17,25},{2,10},{10,18},{18,26},{... | collective-permute-start | bytes 393224 | tf_op jit(solution)/shard_map/ppermute | solution.py:14
  10.6 9.2 %pad_maximum_fusion.4 = (bf16[2,128,64,128]{3,2,1,0:T(8,128)(2,1)}, bf16[2,136,64,128]{3,2,1,0:T(8,128)(2,1)S(1)}, bf16[2,128,64,128]{3,2,1,0:T(8,128)(2,1)S(1)}) fusion(bf16[2,4,64,128]{3,2,1,0:T(8,128)(2,1)S(1)} %collective-permute-done.1, bf16[2,128,64,128]{3,2,1,0:T(8,128)(2,1)} %param.8, ...), kind=kLoop, calls=%fused_computation.43 | loop fusion | flops 16777216 | bytes 17039360 | tf_op jit(solution)/shard_map/concatenate | solution.py:18
  22.8 2.6 broadcast_and_fusion
  27.0 14.7 %pad_maximum_fusion.5 = (bf16[2,128,64,128]{3,2,1,0:T(8,128)(2,1)}, bf16[2,128,64,128]{3,2,1,0:T(8,128)(2,1)}, bf16[2,128,64,128]{3,2,1,0:T(8,128)(2,1)}, bf16[2...) fusion(bf16[2,136,64,128]{3,2,1,0:T(8,128)(2,1)S(1)} %constant_dynamic-u, ...), kind=kLoop, calls=%fused_computation.44 | loop fusion | flops 50331648 | bytes 30179328 | tf_op jit(solution)/shard_map/concatenate | solution.py:18
  46.4 3.4 %convolution_add_fusion.12 = f32[16384,128]{1,0:T(8,128)S(1)} fusion(f32[16384,128]{1,0:T(8,128)S(1)} %convolution_add_fusion.13, bf16[16384,128]{1,0:T(8,128)(2,1)} %bitcast.119, bf16[3,3,128,128]{3,2,1,0:T(8,128)(2,1)S(1)} %copy-done.11), kind=kOutput, calls=%fused_computation.17 | convolution fusion | flops 538968064 | bytes 21004288 | tf_op jit(solution)/shard_map/dot_general | solution.py:34
  49.8 3.6 %convolution_add_fusion.11 = f32[16384,128]{1,0:T(8,128)S(1)} fusion(f32[16384,128]{1,0:T(8,128)S(1)} %convolution_add_fusion.12, bf16[16384,128]{1,0:T(8,128)(2,1)} %bitcast.118, bf16[3,3,128,128]{3,2,1,0:T(8,128)(2,1)S(1)} %copy-done.11), kind=kOutput, calls=%fused_computation.16 | convolution fusion | flops 538968064 | bytes 21004288 | tf_op jit(solution)/shard_map/dot_general | solution.py:34
  55.9 3.4 %convolution_add_fusion.8 = f32[16384,128]{1,0:T(8,128)S(1)} fusion(f32[16384,128]{1,0:T(8,128)S(1)} %convolution_add_fusion.9, bf16[16384,128]{1,0:T(8,128)(2,1)} %bitcast.116, bf16[3,3,128,128]{3,2,1,0:T(8,128)(2,1)S(1)} %copy-done.11), kind=kOutput, calls=%fused_computation.13 | convolution fusion | flops 538968064 | bytes 21004288 | tf_op jit(solution)/shard_map/dot_general | solution.py:34
  59.4 4.1 %fusion.7 = bf16[16384,128]{1,0:T(8,128)(2,1)S(1)} fusion(f32[16384,128]{1,0:T(8,128)S(1)} %fusion.27, f32[16384,128]{1,0:T(8,128)S(1)} %convolution_add_fusion.8, bf16[16384,128]{1,0:T(8,128)(2,1)} %bitcast.125, f32[128]{0:T(128)S(1)} %copy-done.15, bf16[3,3,128,128]{3,2,1,0:T(8,128)(2,1)S(1)} %copy-done.11), kind=kOutput, calls=%fused_computation.22 | convolution fusion | flops 547356672 | bytes 25199104 | tf_op jit(solution)/shard_map/dot_general | solution.py:34
  63.5 2.0 copy-done
  66.8 5.0 %collective-permute-start.4 = (bf16[2,8,64,128]{3,2,1,0:T(8,128)(2,1)S(1)}, bf16[2,8,64,128]{3,2,1,0:T(8,128)(2,1)S(1)}, u32[]{:S(2)}, u32[]{:S(2)}) collective-permute-start(bf16[2,8,64,128]{3,2,1,0:T(8,128)(2,1)S(1)} %get-tuple-element.28), channel_id=1, source_target_pairs={{0,8},{8,16},{16,24},{1,9},{9,17},{17,25},{2,10},{10,18},{18,26},{... | collective-permute-start | bytes 786440 | tf_op jit(solution)/shard_map/ppermute | solution.py:14
  71.8 6.3 %all_gather.3 = bf16[256,128]{1,0:T(8,128)(2,1)S(1)} all-gather(bf16[128,128]{1,0:T(8,128)(2,1)S(1)} %copy-done.13), channel_id=1, replica_groups=mesh['row'=4,'col'=4,'agent'=2] {'agent'}, dimensions={0}, use_global_device_ids=true | all-gather | bytes 98304 | tf_op jit(solution)/shard_map/all_gather | solution.py:53
  80.6 2.9 %collective-permute-start.6 = (bf16[2,144,8,128]{3,2,1,0:T(8,128)(2,1)S(1)}, bf16[2,144,8,128]{3,2,1,0:T(8,128)(2,1)S(1)}, u32[]{:S(2)}, u32[]{:S(2)}) collective-permute-start(bf16[2,144,8,128]{3,2,1,0:T(8,128)(2,1)S(1)} %get-tuple-element.19), channel_id=1, source_target_pairs={{0,1},{1,2},{2,3},{3,4},{4,5},{5,6},{6,7},{8,9},{9,10},{10,11},{11... | collective-permute-start | bytes 1769480 | tf_op jit(solution)/shard_map/ppermute | solution.py:14
  84.9 14.5 %pad_maximum_fusion.1 = (bf16[2,128,64,128]{3,2,1,0:T(8,128)(2,1)}, bf16[2,128,64,128]{3,2,1,0:T(8,128)(2,1)S(1)}) fusion(bf16[2,8,64,128]{3,2,1,0:T(8,128)(2,1)S(1)} %collective-permute-done.5, bf16[2,128,64,128]{3,2,1,0:T(8,128)(2,1)S(1)} %bitcast.105, bf16[2,8,64,128]{3,2,1,0:T(8,128)(2,1)S(1)} %collective-permute-done.4), kind=kLoop, calls=%fused_computation.40 | loop fusion | flops 4194304 | bytes 13107200 | tf_op jit(solution)/shard_map/concatenate | solution.py:18
  99.5 4.6 %fusion.24 = f32[16384,128]{1,0:T(8,128)} fusion(bf16[16384,128]{1,0:T(8,128)(2,1)S(1)} %bitcast.121, bf16[3,3,128,128]{3,2,1,0:T(8,128)(2,1)S(1)} %copy-done.12), kind=kOutput, calls=%fused_computation.64 | convolution fusion | flops 536870912 | bytes 12615680 | tf_op jit(solution)/shard_map/dot_general | solution.py:34
  104.1 7.8 %maximum_maximum_fusion = (bf16[2,144,72,128]{3,2,1,0:T(8,128)(2,1)}, bf16[2,144,72,128]{3,2,1,0:T(8,128)(2,1)}) fusion(bf16[2,8,64,128]{3,2,1,0:T(8,128)(2,1)S(1)} %collective-permute-done.5, bf16[2,128,64,128]{3,2,1,0:T(8,128)(2,1)S(1)} %bitcast.106, bf16[2,8,64,128]{3,2,1,0:T(8,128)(2,1)S(1)} %collective-permute-done.4, ...), kind=kLoop, calls=%fused_computation.30 | loop fusion | flops 42467328 | bytes 16515072 | tf_op jit(solution)/shard_map/concatenate | solution.py:18
  111.9 18.5 %fusion.58 = (bf16[2,128,64,128]{3,2,1,0:T(8,128)(2,1)}, bf16[2,128,64,128]{3,2,1,0:T(8,128)(2,1)}, bf16[2,128,64,128]{3,2,1,0:T(8,128)(2,1)}, bf16[2,128,64,128...) fusion(bf16[2,144,72,128]{3,2,1,0:T(8,128)(2,1)} %get-tuple-element.17, ...), kind=kLoop, calls=%fused_computation.113 | loop fusion | bytes 50331648 | tf_op jit(solution)/shard_map/slice | solution.py:28
  130.4 3.6 %fusion.16 = f32[16384,128]{1,0:T(8,128)S(1)} fusion(bf16[16384,128]{1,0:T(8,128)(2,1)} %bitcast.120, bf16[3,3,128,128]{3,2,1,0:T(8,128)(2,1)S(1)} %copy-done.12), kind=kOutput, calls=%fused_computation.56 | convolution fusion | flops 536870912 | bytes 12615680 | tf_op jit(solution)/shard_map/dot_general | solution.py:34
  144.0 3.6 %convolution_add_fusion.2 = f32[16384,128]{1,0:T(8,128)S(1)} fusion(f32[16384,128]{1,0:T(8,128)S(1)} %convolution_add_fusion.3, bf16[16384,128]{1,0:T(8,128)(2,1)} %bitcast.111, bf16[3,3,128,128]{3,2,1,0:T(8,128)(2,1)S(1)} %copy-done.12), kind=kOutput, calls=%fused_computation.5 | convolution fusion | flops 538968064 | bytes 21004288 | tf_op jit(solution)/shard_map/dot_general | solution.py:34
  148.9 6.2 %fusion.6 = bf16[16384,128]{1,0:T(8,128)(2,1)} fusion(f32[16384,128]{1,0:T(8,128)S(1)} %fusion.16, f32[16384,128]{1,0:T(8,128)S(1)} %convolution_add_fusion.1, bf16[16384,128]{1,0:T(8,128)(2,1)} %bitcast.124, f32[128]{0:T(128)S(1)} %copy-done.16, bf16[3,3,128,128]{3,2,1,0:T(8,128)(2,1)S(1)} %copy-done.12), kind=kOutput, calls=%fused_computation.21 | convolution fusion | flops 547356672 | bytes 25199104 | tf_op jit(solution)/shard_map/dot_general | solution.py:34
  155.1 9.7 %select_reduce_fusion.1 = (f32[2,256]{1,0:T(2,128)S(1)}, f32[2,8192,256]{2,1,0:T(8,128)}) fusion(pred[8192,256]{1,0:T(8,128)(4,1)S(1)} %bitcast.107, bf16[2,8192,128]{2,1,0:T(8,128)(2,1)} %bitcast.126, bf16[256,128]{1,0:T(8,128)(2,1)S(1)} %gather_fusion, pred[256]{0:T(512)(128)(4,1)S(1)} %compare_and_fusion.2), kind=kOutput, calls=%fused_computation.24 | convolution fusion | flops 1082162688 | bytes 23136512 | tf_op jit(solution)/shard_map/snc,ac->sna/dot_general | solution.py:57
  164.8 45.7 %pmax.7 = f32[2,256]{1,0:T(2,128)S(1)} all-reduce(f32[2,256]{1,0:T(2,128)S(1)} %get-tuple-element.39), channel_id=1, replica_groups=mesh['row'=4,'col'=4,'agent'=2] {'row','col','agent'}, use_global_device_ids=true, to_apply=%region_1.2 | all-reduce | flops 512 | bytes 4096 | tf_op jit(solution)/shard_map/pmax | solution.py:68
  210.5 7.6 %select_reduce_fusion = f32[2,256]{1,0:T(2,128)S(1)} fusion(f32[2,8192,256]{2,1,0:T(8,128)} %get-tuple-element.40, f32[2,256]{1,0:T(2,128)S(1)} %pmax.7, pred[8192,256]{1,0:T(8,128)(4,1)S(1)} %bitcast.108), kind=kLoop, calls=%fused_computation.23 | loop fusion | flops 12582400 | bytes 18878464 | tf_op jit(solution)/shard_map/reduce_sum | solution.py:69
  218.1 41.5 %psum.7 = f32[2,256]{1,0:T(2,128)S(1)} all-reduce(f32[2,256]{1,0:T(2,128)S(1)} %select_reduce_fusion), channel_id=1, replica_groups=mesh['row'=4,'col'=4,'agent'=2] {'row','col','agent'}, use_global_device_ids=true, to_apply=%region_3.4 | all-reduce | flops 512 | bytes 4096 | tf_op jit(solution)/shard_map/psum | solution.py:70
  259.6 11.4 %broadcast_subtract_fusion = f32[2,8192,256]{2,1,0:T(8,128)} fusion(f32[2,8192,256]{2,1,0:T(8,128)} %get-tuple-element.40, f32[2,256]{1,0:T(2,128)S(1)} %log_add_fusion), kind=kLoop, calls=%fused_computation.25 | loop fusion | flops 4194304 | bytes 33556480 | tf_op jit(solution)/shard_map/sub | solution.py:72
  (76 shorter events, 33.0 us)
Async XLA Ops:
  1.0 9.6 %collective-permute-start.1 = (bf16[2,4,64,128]{3,2,1,0:T(8,128)(2,1)S(1)}, bf16[2,4,64,128]{3,2,1,0:T(8,128)(2,1)S(1)}, u32[]{:S(2)}, u32[]{:S(2)}) collective-permute-start(bf16[2,4,64,128]{3,2,1,0:T(8,128)(2,1)S(1)} %get-tuple-element.33), channel_id=1, source_target_pairs={{8,0},{16,8},{24,16},{9,1},{17,9},{25,17},{10,2},{18,10},{26,18},{... | collective-permute-start | bytes 393224 | tf_op jit(solution)/shard_map/ppermute | solution.py:17
  2.3 8.3 %collective-permute-start = (bf16[2,4,64,128]{3,2,1,0:T(8,128)(2,1)S(1)}, bf16[2,4,64,128]{3,2,1,0:T(8,128)(2,1)S(1)}, u32[]{:S(2)}, u32[]{:S(2)}) collective-permute-start(bf16[2,4,64,128]{3,2,1,0:T(8,128)(2,1)S(1)} %get-tuple-element.34), channel_id=1, source_target_pairs={{0,8},{8,16},{16,24},{1,9},{9,17},{17,25},{2,10},{10,18},{18,26},{... | collective-permute-start | bytes 393224 | tf_op jit(solution)/shard_map/ppermute | solution.py:14
  19.9 5.6 %copy-start.14 = (s32[256]{0:T(256)S(1)}, s32[256]{0:T(256)}, u32[]{:S(2)}) copy-start(s32[256]{0:T(256)} %param.14) | copy-start | bytes 3076
  20.2 5.3 %collective-permute-start.2 = (bf16[2,136,4,128]{3,1,2,0:T(8,128)(2,1)S(1)}, bf16[2,136,4,128]{3,1,2,0:T(8,128)(2,1)S(1)}, u32[]{:S(2)}, u32[]{:S(2)}) collective-permute-start(bf16[2,136,4,128]{3,1,2,0:T(8,128)(2,1)S(1)} %copy.14), channel_id=1, source_target_pairs={{0,1},{1,2},{2,3},{3,4},{4,5},{5,6},{6,7},{8,9},{9,10},{10,11},{11... | collective-permute-start | bytes 835592 | tf_op jit(solution)/shard_map/ppermute | solution.py:14
  21.5 5.4 %collective-permute-start.3 = (bf16[2,136,4,128]{3,1,2,0:T(8,128)(2,1)S(1)}, bf16[2,136,4,128]{3,1,2,0:T(8,128)(2,1)S(1)}, u32[]{:S(2)}, u32[]{:S(2)}) collective-permute-start(bf16[2,136,4,128]{3,1,2,0:T(8,128)(2,1)S(1)} %copy.16), channel_id=1, source_target_pairs={{1,0},{2,1},{3,2},{4,3},{5,4},{6,5},{7,6},{9,8},{10,9},{11,10},{12... | collective-permute-start | bytes 835592 | tf_op jit(solution)/shard_map/ppermute | solution.py:17
  27.0 14.7 %copy-start.11 = (bf16[3,3,128,128]{3,2,1,0:T(8,128)(2,1)S(1)}, bf16[3,3,128,128]{3,2,1,0:T(8,128)(2,1)}, u32[]{:S(2)}) copy-start(bf16[3,3,128,128]{3,2,1,0:T(8,128)(2,1)} %param.9) | copy-start | bytes 884740
  41.7 2.2 copy-start.10
  49.8 3.6 %copy-start.5 = (bf16[2,128,64,128]{3,2,1,0:T(8,128)(2,1)S(1)}, bf16[2,128,64,128]{3,2,1,0:T(8,128)(2,1)}, u32[]{:S(2)}) copy-start(bf16[2,128,64,128]{3,2,1,0:T(8,128)(2,1)} %param.8) | copy-start | bytes 12582916
  55.9 3.4 %copy-start.15 = (f32[128]{0:T(128)S(1)}, f32[128]{0:T(128)}, u32[]{:S(2)}) copy-start(f32[128]{0:T(128)} %param.10) | copy-start | bytes 1540
  59.4 12.5 %copy-start.13 = (bf16[128,128]{1,0:T(8,128)(2,1)S(1)}, bf16[128,128]{1,0:T(8,128)(2,1)}, u32[]{:S(2)}) copy-start(bf16[128,128]{1,0:T(8,128)(2,1)} %param.13) | copy-start | bytes 98308
  63.5 2.0 copy-start
  65.5 13.5 %collective-permute-start.5 = (bf16[2,8,64,128]{3,2,1,0:T(8,128)(2,1)S(1)}, bf16[2,8,64,128]{3,2,1,0:T(8,128)(2,1)S(1)}, u32[]{:S(2)}, u32[]{:S(2)}) collective-permute-start(bf16[2,8,64,128]{3,2,1,0:T(8,128)(2,1)S(1)} %get-tuple-element.29), channel_id=1, source_target_pairs={{8,0},{16,8},{24,16},{9,1},{17,9},{25,17},{10,2},{18,10},{26,18},{... | collective-permute-start | bytes 786440 | tf_op jit(solution)/shard_map/ppermute | solution.py:17
  66.8 12.2 %collective-permute-start.4 = (bf16[2,8,64,128]{3,2,1,0:T(8,128)(2,1)S(1)}, bf16[2,8,64,128]{3,2,1,0:T(8,128)(2,1)S(1)}, u32[]{:S(2)}, u32[]{:S(2)}) collective-permute-start(bf16[2,8,64,128]{3,2,1,0:T(8,128)(2,1)S(1)} %get-tuple-element.28), channel_id=1, source_target_pairs={{0,8},{8,16},{16,24},{1,9},{9,17},{17,25},{2,10},{10,18},{18,26},{... | collective-permute-start | bytes 786440 | tf_op jit(solution)/shard_map/ppermute | solution.py:14
  79.0 5.9 %copy-start.1 = (bf16[16384,128]{1,0:T(8,128)(2,1)S(1)}, bf16[16384,128]{1,0:T(8,128)(2,1)}, u32[]{:S(2)}) copy-start(bf16[16384,128]{1,0:T(8,128)(2,1)} %copy-done) | copy-start | bytes 12582916
  80.6 23.5 %collective-permute-start.6 = (bf16[2,144,8,128]{3,2,1,0:T(8,128)(2,1)S(1)}, bf16[2,144,8,128]{3,2,1,0:T(8,128)(2,1)S(1)}, u32[]{:S(2)}, u32[]{:S(2)}) collective-permute-start(bf16[2,144,8,128]{3,2,1,0:T(8,128)(2,1)S(1)} %get-tuple-element.19), channel_id=1, source_target_pairs={{0,1},{1,2},{2,3},{3,4},{4,5},{5,6},{6,7},{8,9},{9,10},{10,11},{11... | collective-permute-start | bytes 1769480 | tf_op jit(solution)/shard_map/ppermute | solution.py:14
  83.5 16.0 %copy-start.12 = (bf16[3,3,128,128]{3,2,1,0:T(8,128)(2,1)S(1)}, bf16[3,3,128,128]{3,2,1,0:T(8,128)(2,1)}, u32[]{:S(2)}) copy-start(bf16[3,3,128,128]{3,2,1,0:T(8,128)(2,1)} %param.11) | copy-start | bytes 884740
  83.5 20.6 %collective-permute-start.7 = (bf16[2,144,8,128]{3,2,1,0:T(8,128)(2,1)S(1)}, bf16[2,144,8,128]{3,2,1,0:T(8,128)(2,1)S(1)}, u32[]{:S(2)}, u32[]{:S(2)}) collective-permute-start(bf16[2,144,8,128]{3,2,1,0:T(8,128)(2,1)S(1)} %get-tuple-element.20), channel_id=1, source_target_pairs={{1,0},{2,1},{3,2},{4,3},{5,4},{6,5},{7,6},{9,8},{10,9},{11,10},{12... | collective-permute-start | bytes 1769480 | tf_op jit(solution)/shard_map/ppermute | solution.py:17
  130.4 4.6 %copy-start.3 = (f32[16384,128]{1,0:T(8,128)S(1)}, f32[16384,128]{1,0:T(8,128)}, u32[]{:S(2)}) copy-start(f32[16384,128]{1,0:T(8,128)} %fusion.24) | copy-start | bytes 25165828
  130.4 5.8 %copy-start.9 = (bf16[2,128,64,128]{3,2,1,0:T(8,128)(2,1)S(1)}, bf16[2,128,64,128]{3,2,1,0:T(8,128)(2,1)}, u32[]{:S(2)}) copy-start(bf16[2,128,64,128]{3,2,1,0:T(8,128)(2,1)} %get-tuple-element.7) | copy-start | bytes 12582916
  136.2 2.2 copy-start.8
  138.4 2.2 copy-start.7
  140.6 2.2 copy-start.2
  144.0 3.6 %copy-start.6 = (bf16[2,128,64,128]{3,2,1,0:T(8,128)(2,1)S(1)}, bf16[2,128,64,128]{3,2,1,0:T(8,128)(2,1)}, u32[]{:S(2)}) copy-start(bf16[2,128,64,128]{3,2,1,0:T(8,128)(2,1)} %get-tuple-element.5) | copy-start | bytes 12582916
  148.9 6.2 %copy-start.4 = (pred[128,64,256]{2,1,0:T(8,128)(4,1)S(1)}, pred[128,64,256]{2,1,0:T(8,128)(4,1)}, u32[]{:S(2)}) copy-start(pred[128,64,256]{2,1,0:T(8,128)(4,1)} %broadcast_and_fusion) | copy-start | bytes 6291460
  (1 other events, 1.3 us)
where the time goes:
time: 277 us; the launch traced here: 271 us
  blocking collectives  93.5 us (34%)
  other arithmetic  69.7 us (25%)
  matrix products  54.6 us (20%)
  local copies, waits for them, and re-layouts  29.8 us (11%)
  starting transfers between devices  20.1 us (7%)
  waiting for transfers between devices  2.99 us (1%)
    concatenate x4, other arithmetic, padded_2(): block = jnp.concatenate([low, block, high], axis=dim)  46.2 us
    pmax x1, blocking collectives, shards(): peak = lax.pmax(local_peak, ('row', 'col', 'agent'))  45.7 us
    dot_general x18, matrix products, dilated(): jnp.dot(tap_piece.reshape(-1, channels), kernel[row_tap, col_tap], prefer...  44.9 us
    psum x1, blocking collectives, shards(): mass = lax.psum(local_mass, ('row', 'col', 'agent'))  41.5 us
    slice x1, local copies, waits for them, and re-layouts, dilated(): padded[:, row_tap * dilation:row_tap * dilation + out_rows, col_tap * dil...  18.5 us
    ppermute x4, starting transfers between devices, padded_2(): lax.ppermute(lax.slice_in_dim(block, block.shape[dim] - width, None, axis...  14.8 us
    sub x1, other arithmetic, shards(): logits - normaliser[:, None, :]  11.4 us
    dot_general x1, matrix products, shards(): jnp.einsum('snc,ac->sna', flat, ordered, preferred_element_type=jnp.float32)  9.68 us
  transfers between devices with their start and end apart: 8, of which 2 were waited for; matrix products, arithmetic and copies ran while one was open for 9% of the time, Pallas kernels for 0%

commit v1 on v0

--- a/solution.py
+++ b/solution.py
@@ -67,7 +67,7 @@
     local_peak = jnp.max(jnp.where(valid, logits, -1e30), axis=1)
     peak = lax.pmax(local_peak, ("row", "col", "agent"))
     local_mass = jnp.sum(jnp.where(valid, jnp.exp(logits - peak[:, None, :]), 0.0), axis=1)
-    mass = lax.psum(local_mass, ("row", "col", "agent"))
+    mass = jnp.sum(lax.all_gather(local_mass, ("row", "col", "agent")), axis=0)
     normaliser = peak + jnp.log(mass)
     return (logits - normaliser[:, None, :]).reshape(scenes, tile_rows, tile_cols, agents)
 

time: 277 us -> 268 us (0.968)
  other arithmetic: 69.7 us -> 57.6 us
  blocking collectives: 93.5 us -> 96.8 us
    all_gather x0 -> x1, blocking collectives: none -> 41.6 us  [shards(): mass = jnp.sum(lax.all_gather(local_mass, ('row', 'col', 'agent')), axis=0)]
    psum x1 -> x0, blocking collectives: 41.5 us -> none  [shards(): mass = lax.psum(local_mass, ('row', 'col', 'agent'))]
    concatenate x4, other arithmetic: 46.2 us -> 34.1 us  [padded_2(): block = jnp.concatenate([low, block, high], axis=dim)]
    pmax x1, blocking collectives: 45.7 us -> 48.9 us  [shards(): peak = lax.pmax(local_peak, ('row', 'col', 'agent'))]
  transfers between devices with their start and end apart: 8 -> 8, of which waited for: 2 -> 2; matrix products, arithmetic and copies ran while one was open for 9% -> 5% of each run, Pallas kernels for 0% -> 0%
where the time goes in v1:
time: 268 us; the launch traced here: 263 us
  blocking collectives  96.8 us (36%)
  other arithmetic  57.6 us (21%)
  matrix products  54.6 us (20%)
  local copies, waits for them, and re-layouts  29.8 us (11%)
  starting transfers between devices  20.1 us (8%)
  waiting for transfers between devices  2.99 us (1%)
    pmax x1, blocking collectives, shards(): peak = lax.pmax(local_peak, ('row', 'col', 'agent'))  48.9 us
    dot_general x18, matrix products, dilated(): jnp.dot(tap_piece.reshape(-1, channels), kernel[row_tap, col_tap], prefer...  44.9 us
    all_gather x1, blocking collectives, shards(): mass = jnp.sum(lax.all_gather(local_mass, ('row', 'col', 'agent')), axis=0)  41.6 us
    concatenate x4, other arithmetic, padded_2(): block = jnp.concatenate([low, block, high], axis=dim)  34.1 us
    slice x1, local copies, waits for them, and re-layouts, dilated(): padded[:, row_tap * dilation:row_tap * dilation + out_rows, col_tap * dil...  18.5 us
    ppermute x4, starting transfers between devices, padded_2(): lax.ppermute(lax.slice_in_dim(block, block.shape[dim] - width, None, axis...  14.8 us
    sub x1, other arithmetic, shards(): logits - normaliser[:, None, :]  11.4 us
    dot_general x1, matrix products, shards(): jnp.einsum('snc,ac->sna', flat, ordered, preferred_element_type=jnp.float32)  9.69 us
  transfers between devices with their start and end apart: 8, of which 2 were waited for; matrix products, arithmetic and copies ran while one was open for 5% of the time, Pallas kernels for 0%

profile of v1, /device:TPU:0, one launch (start us, length us, event | category | flops | bytes accessed | tf_op | source)
XLA Modules:
  0.0 262.7 jit_solution(15597294999027113523)
XLA Ops:
  2.3 5.6 %collective-permute-start = (bf16[2,4,64,128]{3,2,1,0:T(8,128)(2,1)S(1)}, bf16[2,4,64,128]{3,2,1,0:T(8,128)(2,1)S(1)}, u32[]{:S(2)}, u32[]{:S(2)}) collective-permute-start(bf16[2,4,64,128]{3,2,1,0:T(8,128)(2,1)S(1)} %get-tuple-element.34), channel_id=1, source_target_pairs={{0,8},{8,16},{16,24},{1,9},{9,17},{17,25},{2,10},{10,18},{18,26},{... | collective-permute-start | bytes 393224 | tf_op jit(solution)/shard_map/ppermute | solution.py:14
  10.6 9.2 %pad_maximum_fusion.4 = (bf16[2,128,64,128]{3,2,1,0:T(8,128)(2,1)}, bf16[2,136,64,128]{3,2,1,0:T(8,128)(2,1)S(1)}, bf16[2,128,64,128]{3,2,1,0:T(8,128)(2,1)S(1)}) fusion(bf16[2,4,64,128]{3,2,1,0:T(8,128)(2,1)S(1)} %collective-permute-done.1, bf16[2,128,64,128]{3,2,1,0:T(8,128)(2,1)} %param.8, ...), kind=kLoop, calls=%fused_computation.43 | loop fusion | flops 16777216 | bytes 17039360 | tf_op jit(solution)/shard_map/concatenate | solution.py:18
  22.8 2.6 %broadcast_and_fusion = pred[128,64,256]{2,1,0:T(8,128)(4,1)} fusion(pred[64,256]{1,0:T(8,128)(4,1)S(1)} %compare_and_fusion.1, pred[128,256]{1,0:T(8,128)(4,1)S(1)} %compare_and_fusion), kind=kLoop, calls=%fused_computation.46 | loop fusion | flops 2097152 | bytes 2146304 | tf_op jit(solution)/shard_map/and | solution.py:66
  27.0 14.5 %pad_maximum_fusion.5 = (bf16[2,128,64,128]{3,2,1,0:T(8,128)(2,1)}, bf16[2,128,64,128]{3,2,1,0:T(8,128)(2,1)}, bf16[2,128,64,128]{3,2,1,0:T(8,128)(2,1)}, bf16[2...) fusion(bf16[2,136,64,128]{3,2,1,0:T(8,128)(2,1)S(1)} %constant_dynamic-u, ...), kind=kLoop, calls=%fused_computation.44 | loop fusion | flops 50331648 | bytes 30179328 | tf_op jit(solution)/shard_map/concatenate | solution.py:18
  46.2 3.4 %convolution_add_fusion.12 = f32[16384,128]{1,0:T(8,128)S(1)} fusion(f32[16384,128]{1,0:T(8,128)S(1)} %convolution_add_fusion.13, bf16[16384,128]{1,0:T(8,128)(2,1)} %bitcast.120, bf16[3,3,128,128]{3,2,1,0:T(8,128)(2,1)S(1)} %copy-done.11), kind=kOutput, calls=%fused_computation.17 | convolution fusion | flops 538968064 | bytes 21004288 | tf_op jit(solution)/shard_map/dot_general | solution.py:34
  49.6 3.6 %convolution_add_fusion.11 = f32[16384,128]{1,0:T(8,128)S(1)} fusion(f32[16384,128]{1,0:T(8,128)S(1)} %convolution_add_fusion.12, bf16[16384,128]{1,0:T(8,128)(2,1)} %bitcast.119, bf16[3,3,128,128]{3,2,1,0:T(8,128)(2,1)S(1)} %copy-done.11), kind=kOutput, calls=%fused_computation.16 | convolution fusion | flops 538968064 | bytes 21004288 | tf_op jit(solution)/shard_map/dot_general | solution.py:34
  55.7 3.4 %convolution_add_fusion.8 = f32[16384,128]{1,0:T(8,128)S(1)} fusion(f32[16384,128]{1,0:T(8,128)S(1)} %convolution_add_fusion.9, bf16[16384,128]{1,0:T(8,128)(2,1)} %bitcast.117, bf16[3,3,128,128]{3,2,1,0:T(8,128)(2,1)S(1)} %copy-done.11), kind=kOutput, calls=%fused_computation.13 | convolution fusion | flops 538968064 | bytes 21004288 | tf_op jit(solution)/shard_map/dot_general | solution.py:34
  59.2 4.1 %fusion.7 = bf16[16384,128]{1,0:T(8,128)(2,1)S(1)} fusion(f32[16384,128]{1,0:T(8,128)S(1)} %fusion.27, f32[16384,128]{1,0:T(8,128)S(1)} %convolution_add_fusion.8, bf16[16384,128]{1,0:T(8,128)(2,1)} %bitcast.126, f32[128]{0:T(128)S(1)} %copy-done.15, bf16[3,3,128,128]{3,2,1,0:T(8,128)(2,1)S(1)} %copy-done.11), kind=kOutput, calls=%fused_computation.22 | convolution fusion | flops 547356672 | bytes 25199104 | tf_op jit(solution)/shard_map/dot_general | solution.py:34
  63.3 2.0 copy-done
  66.6 5.0 %collective-permute-start.4 = (bf16[2,8,64,128]{3,2,1,0:T(8,128)(2,1)S(1)}, bf16[2,8,64,128]{3,2,1,0:T(8,128)(2,1)S(1)}, u32[]{:S(2)}, u32[]{:S(2)}) collective-permute-start(bf16[2,8,64,128]{3,2,1,0:T(8,128)(2,1)S(1)} %get-tuple-element.28), channel_id=1, source_target_pairs={{0,8},{8,16},{16,24},{1,9},{9,17},{17,25},{2,10},{10,18},{18,26},{... | collective-permute-start | bytes 786440 | tf_op jit(solution)/shard_map/ppermute | solution.py:14
  71.6 6.3 %all_gather.9 = bf16[256,128]{1,0:T(8,128)(2,1)S(1)} all-gather(bf16[128,128]{1,0:T(8,128)(2,1)S(1)} %copy-done.13), channel_id=1, replica_groups=mesh['row'=4,'col'=4,'agent'=2] {'agent'}, dimensions={0}, use_global_device_ids=true | all-gather | bytes 98304 | tf_op jit(solution)/shard_map/all_gather | solution.py:53
  80.4 2.9 %collective-permute-start.6 = (bf16[2,144,8,128]{3,2,1,0:T(8,128)(2,1)S(1)}, bf16[2,144,8,128]{3,2,1,0:T(8,128)(2,1)S(1)}, u32[]{:S(2)}, u32[]{:S(2)}) collective-permute-start(bf16[2,144,8,128]{3,2,1,0:T(8,128)(2,1)S(1)} %get-tuple-element.19), channel_id=1, source_target_pairs={{0,1},{1,2},{2,3},{3,4},{4,5},{5,6},{6,7},{8,9},{9,10},{10,11},{11... | collective-permute-start | bytes 1769480 | tf_op jit(solution)/shard_map/ppermute | solution.py:14
  84.7 2.7 %pad_maximum_fusion.1 = (bf16[2,128,64,128]{3,2,1,0:T(8,128)(2,1)}, bf16[2,128,64,128]{3,2,1,0:T(8,128)(2,1)S(1)}) fusion(bf16[2,8,64,128]{3,2,1,0:T(8,128)(2,1)S(1)} %collective-permute-done.5, bf16[2,128,64,128]{3,2,1,0:T(8,128)(2,1)S(1)} %bitcast.106, bf16[2,8,64,128]{3,2,1,0:T(8,128)(2,1)S(1)} %collective-permute-done.4), kind=kLoop, calls=%fused_computation.40 | loop fusion | flops 4194304 | bytes 13107200 | tf_op jit(solution)/shard_map/concatenate | solution.py:18
  87.4 4.6 %fusion.24 = f32[16384,128]{1,0:T(8,128)} fusion(bf16[16384,128]{1,0:T(8,128)(2,1)S(1)} %bitcast.122, bf16[3,3,128,128]{3,2,1,0:T(8,128)(2,1)S(1)} %copy-done.12), kind=kOutput, calls=%fused_computation.64 | convolution fusion | flops 536870912 | bytes 12615680 | tf_op jit(solution)/shard_map/dot_general | solution.py:34
  92.0 7.8 %maximum_maximum_fusion = (bf16[2,144,72,128]{3,2,1,0:T(8,128)(2,1)}, bf16[2,144,72,128]{3,2,1,0:T(8,128)(2,1)}) fusion(bf16[2,8,64,128]{3,2,1,0:T(8,128)(2,1)S(1)} %collective-permute-done.5, bf16[2,128,64,128]{3,2,1,0:T(8,128)(2,1)S(1)} %bitcast.107, bf16[2,8,64,128]{3,2,1,0:T(8,128)(2,1)S(1)} %collective-permute-done.4, ...), kind=kLoop, calls=%fused_computation.30 | loop fusion | flops 42467328 | bytes 16515072 | tf_op jit(solution)/shard_map/concatenate | solution.py:18
  99.8 18.5 %fusion.58 = (bf16[2,128,64,128]{3,2,1,0:T(8,128)(2,1)}, bf16[2,128,64,128]{3,2,1,0:T(8,128)(2,1)}, bf16[2,128,64,128]{3,2,1,0:T(8,128)(2,1)}, bf16[2,128,64,128...) fusion(bf16[2,144,72,128]{3,2,1,0:T(8,128)(2,1)} %get-tuple-element.17, ...), kind=kLoop, calls=%fused_computation.113 | loop fusion | bytes 50331648 | tf_op jit(solution)/shard_map/slice | solution.py:28
  118.3 3.6 %fusion.16 = f32[16384,128]{1,0:T(8,128)S(1)} fusion(bf16[16384,128]{1,0:T(8,128)(2,1)} %bitcast.121, bf16[3,3,128,128]{3,2,1,0:T(8,128)(2,1)S(1)} %copy-done.12), kind=kOutput, calls=%fused_computation.56 | convolution fusion | flops 536870912 | bytes 12615680 | tf_op jit(solution)/shard_map/dot_general | solution.py:34
  132.0 3.6 %convolution_add_fusion.2 = f32[16384,128]{1,0:T(8,128)S(1)} fusion(f32[16384,128]{1,0:T(8,128)S(1)} %convolution_add_fusion.3, bf16[16384,128]{1,0:T(8,128)(2,1)} %bitcast.112, bf16[3,3,128,128]{3,2,1,0:T(8,128)(2,1)S(1)} %copy-done.12), kind=kOutput, calls=%fused_computation.5 | convolution fusion | flops 538968064 | bytes 21004288 | tf_op jit(solution)/shard_map/dot_general | solution.py:34
  136.8 6.2 %fusion.6 = bf16[16384,128]{1,0:T(8,128)(2,1)} fusion(f32[16384,128]{1,0:T(8,128)S(1)} %fusion.16, f32[16384,128]{1,0:T(8,128)S(1)} %convolution_add_fusion.1, bf16[16384,128]{1,0:T(8,128)(2,1)} %bitcast.125, f32[128]{0:T(128)S(1)} %copy-done.16, bf16[3,3,128,128]{3,2,1,0:T(8,128)(2,1)S(1)} %copy-done.12), kind=kOutput, calls=%fused_computation.21 | convolution fusion | flops 547356672 | bytes 25199104 | tf_op jit(solution)/shard_map/dot_general | solution.py:34
  143.1 9.7 %select_reduce_fusion.1 = (f32[2,256]{1,0:T(2,128)S(1)}, f32[2,8192,256]{2,1,0:T(8,128)}) fusion(pred[8192,256]{1,0:T(8,128)(4,1)S(1)} %bitcast.108, bf16[2,8192,128]{2,1,0:T(8,128)(2,1)} %bitcast.127, bf16[256,128]{1,0:T(8,128)(2,1)S(1)} %gather_fusion, pred[256]{0:T(512)(128)(4,1)S(1)} %compare_and_fusion.2), kind=kOutput, calls=%fused_computation.24 | convolution fusion | flops 1082162688 | bytes 23136512 | tf_op jit(solution)/shard_map/snc,ac->sna/dot_general | solution.py:57
  152.7 48.9 %pmax.7 = f32[2,256]{1,0:T(2,128)S(1)} all-reduce(f32[2,256]{1,0:T(2,128)S(1)} %get-tuple-element.39), channel_id=1, replica_groups=mesh['row'=4,'col'=4,'agent'=2] {'row','col','agent'}, use_global_device_ids=true, to_apply=%region_1.2 | all-reduce | flops 512 | bytes 4096 | tf_op jit(solution)/shard_map/pmax | solution.py:68
  201.6 7.6 %select_reduce_fusion = f32[2,256]{1,0:T(2,128)S(1)} fusion(f32[2,8192,256]{2,1,0:T(8,128)} %get-tuple-element.40, f32[2,256]{1,0:T(2,128)S(1)} %pmax.7, pred[8192,256]{1,0:T(8,128)(4,1)S(1)} %bitcast.109), kind=kLoop, calls=%fused_computation.23 | loop fusion | flops 12582400 | bytes 18878464 | tf_op jit(solution)/shard_map/reduce_sum | solution.py:69
  209.3 41.6 %all-gather.1 = f32[32,2,256]{2,1,0:T(2,128)S(1)} all-gather(f32[1,2,256]{2,1,0:T(2,128)S(1)} %bitcast.128), channel_id=2, replica_groups=mesh['row'=4,'col'=4,'agent'=2] {'row','col','agent'}, dimensions={0}, use_global_device_ids=true | all-gather | bytes 67584 | tf_op jit(solution)/shard_map/all_gather | solution.py:70
  250.9 11.4 %broadcast_subtract_fusion = f32[2,8192,256]{2,1,0:T(8,128)} fusion(f32[2,8192,256]{2,1,0:T(8,128)} %get-tuple-element.40, f32[2,256]{1,0:T(2,128)S(1)} %log_add_fusion), kind=kLoop, calls=%fused_computation.25 | loop fusion | flops 4194304 | bytes 33556480 | tf_op jit(solution)/shard_map/sub | solution.py:72
  (77 shorter events, 33.1 us)
Async XLA Ops:
  1.0 9.6 %collective-permute-start.1 = (bf16[2,4,64,128]{3,2,1,0:T(8,128)(2,1)S(1)}, bf16[2,4,64,128]{3,2,1,0:T(8,128)(2,1)S(1)}, u32[]{:S(2)}, u32[]{:S(2)}) collective-permute-start(bf16[2,4,64,128]{3,2,1,0:T(8,128)(2,1)S(1)} %get-tuple-element.33), channel_id=1, source_target_pairs={{8,0},{16,8},{24,16},{9,1},{17,9},{25,17},{10,2},{18,10},{26,18},{... | collective-permute-start | bytes 393224 | tf_op jit(solution)/shard_map/ppermute | solution.py:17
  2.3 8.3 %collective-permute-start = (bf16[2,4,64,128]{3,2,1,0:T(8,128)(2,1)S(1)}, bf16[2,4,64,128]{3,2,1,0:T(8,128)(2,1)S(1)}, u32[]{:S(2)}, u32[]{:S(2)}) collective-permute-start(bf16[2,4,64,128]{3,2,1,0:T(8,128)(2,1)S(1)} %get-tuple-element.34), channel_id=1, source_target_pairs={{0,8},{8,16},{16,24},{1,9},{9,17},{17,25},{2,10},{10,18},{18,26},{... | collective-permute-start | bytes 393224 | tf_op jit(solution)/shard_map/ppermute | solution.py:14
  19.9 5.6 %copy-start.14 = (s32[256]{0:T(256)S(1)}, s32[256]{0:T(256)}, u32[]{:S(2)}) copy-start(s32[256]{0:T(256)} %param.14) | copy-start | bytes 3076
  20.2 5.3 %collective-permute-start.2 = (bf16[2,136,4,128]{3,1,2,0:T(8,128)(2,1)S(1)}, bf16[2,136,4,128]{3,1,2,0:T(8,128)(2,1)S(1)}, u32[]{:S(2)}, u32[]{:S(2)}) collective-permute-start(bf16[2,136,4,128]{3,1,2,0:T(8,128)(2,1)S(1)} %copy.14), channel_id=1, source_target_pairs={{0,1},{1,2},{2,3},{3,4},{4,5},{5,6},{6,7},{8,9},{9,10},{10,11},{11... | collective-permute-start | bytes 835592 | tf_op jit(solution)/shard_map/ppermute | solution.py:14
  21.5 5.4 %collective-permute-start.3 = (bf16[2,136,4,128]{3,1,2,0:T(8,128)(2,1)S(1)}, bf16[2,136,4,128]{3,1,2,0:T(8,128)(2,1)S(1)}, u32[]{:S(2)}, u32[]{:S(2)}) collective-permute-start(bf16[2,136,4,128]{3,1,2,0:T(8,128)(2,1)S(1)} %copy.16), channel_id=1, source_target_pairs={{1,0},{2,1},{3,2},{4,3},{5,4},{6,5},{7,6},{9,8},{10,9},{11,10},{12... | collective-permute-start | bytes 835592 | tf_op jit(solution)/shard_map/ppermute | solution.py:17
  27.0 14.5 %copy-start.11 = (bf16[3,3,128,128]{3,2,1,0:T(8,128)(2,1)S(1)}, bf16[3,3,128,128]{3,2,1,0:T(8,128)(2,1)}, u32[]{:S(2)}) copy-start(bf16[3,3,128,128]{3,2,1,0:T(8,128)(2,1)} %param.9) | copy-start | bytes 884740
  41.5 2.2 copy-start.10
  49.6 3.6 %copy-start.5 = (bf16[2,128,64,128]{3,2,1,0:T(8,128)(2,1)S(1)}, bf16[2,128,64,128]{3,2,1,0:T(8,128)(2,1)}, u32[]{:S(2)}) copy-start(bf16[2,128,64,128]{3,2,1,0:T(8,128)(2,1)} %param.8) | copy-start | bytes 12582916
  55.7 3.4 %copy-start.15 = (f32[128]{0:T(128)S(1)}, f32[128]{0:T(128)}, u32[]{:S(2)}) copy-start(f32[128]{0:T(128)} %param.10) | copy-start | bytes 1540
  59.2 12.5 %copy-start.13 = (bf16[128,128]{1,0:T(8,128)(2,1)S(1)}, bf16[128,128]{1,0:T(8,128)(2,1)}, u32[]{:S(2)}) copy-start(bf16[128,128]{1,0:T(8,128)(2,1)} %param.13) | copy-start | bytes 98308
  63.3 2.0 copy-start
  65.3 13.5 %collective-permute-start.5 = (bf16[2,8,64,128]{3,2,1,0:T(8,128)(2,1)S(1)}, bf16[2,8,64,128]{3,2,1,0:T(8,128)(2,1)S(1)}, u32[]{:S(2)}, u32[]{:S(2)}) collective-permute-start(bf16[2,8,64,128]{3,2,1,0:T(8,128)(2,1)S(1)} %get-tuple-element.29), channel_id=1, source_target_pairs={{8,0},{16,8},{24,16},{9,1},{17,9},{25,17},{10,2},{18,10},{26,18},{... | collective-permute-start | bytes 786440 | tf_op jit(solution)/shard_map/ppermute | solution.py:17
  66.6 12.2 %collective-permute-start.4 = (bf16[2,8,64,128]{3,2,1,0:T(8,128)(2,1)S(1)}, bf16[2,8,64,128]{3,2,1,0:T(8,128)(2,1)S(1)}, u32[]{:S(2)}, u32[]{:S(2)}) collective-permute-start(bf16[2,8,64,128]{3,2,1,0:T(8,128)(2,1)S(1)} %get-tuple-element.28), channel_id=1, source_target_pairs={{0,8},{8,16},{16,24},{1,9},{9,17},{17,25},{2,10},{10,18},{18,26},{... | collective-permute-start | bytes 786440 | tf_op jit(solution)/shard_map/ppermute | solution.py:14
  78.8 5.9 %copy-start.1 = (bf16[16384,128]{1,0:T(8,128)(2,1)S(1)}, bf16[16384,128]{1,0:T(8,128)(2,1)}, u32[]{:S(2)}) copy-start(bf16[16384,128]{1,0:T(8,128)(2,1)} %copy-done) | copy-start | bytes 12582916
  80.4 11.7 %collective-permute-start.6 = (bf16[2,144,8,128]{3,2,1,0:T(8,128)(2,1)S(1)}, bf16[2,144,8,128]{3,2,1,0:T(8,128)(2,1)S(1)}, u32[]{:S(2)}, u32[]{:S(2)}) collective-permute-start(bf16[2,144,8,128]{3,2,1,0:T(8,128)(2,1)S(1)} %get-tuple-element.19), channel_id=1, source_target_pairs={{0,1},{1,2},{2,3},{3,4},{4,5},{5,6},{6,7},{8,9},{9,10},{10,11},{11... | collective-permute-start | bytes 1769480 | tf_op jit(solution)/shard_map/ppermute | solution.py:14
  83.3 4.1 %copy-start.12 = (bf16[3,3,128,128]{3,2,1,0:T(8,128)(2,1)S(1)}, bf16[3,3,128,128]{3,2,1,0:T(8,128)(2,1)}, u32[]{:S(2)}) copy-start(bf16[3,3,128,128]{3,2,1,0:T(8,128)(2,1)} %param.11) | copy-start | bytes 884740
  83.3 8.7 %collective-permute-start.7 = (bf16[2,144,8,128]{3,2,1,0:T(8,128)(2,1)S(1)}, bf16[2,144,8,128]{3,2,1,0:T(8,128)(2,1)S(1)}, u32[]{:S(2)}, u32[]{:S(2)}) collective-permute-start(bf16[2,144,8,128]{3,2,1,0:T(8,128)(2,1)S(1)} %get-tuple-element.20), channel_id=1, source_target_pairs={{1,0},{2,1},{3,2},{4,3},{5,4},{6,5},{7,6},{9,8},{10,9},{11,10},{12... | collective-permute-start | bytes 1769480 | tf_op jit(solution)/shard_map/ppermute | solution.py:17
  118.3 4.6 %copy-start.3 = (f32[16384,128]{1,0:T(8,128)S(1)}, f32[16384,128]{1,0:T(8,128)}, u32[]{:S(2)}) copy-start(f32[16384,128]{1,0:T(8,128)} %fusion.24) | copy-start | bytes 25165828
  118.3 5.8 %copy-start.9 = (bf16[2,128,64,128]{3,2,1,0:T(8,128)(2,1)S(1)}, bf16[2,128,64,128]{3,2,1,0:T(8,128)(2,1)}, u32[]{:S(2)}) copy-start(bf16[2,128,64,128]{3,2,1,0:T(8,128)(2,1)} %get-tuple-element.7) | copy-start | bytes 12582916
  124.1 2.2 copy-start.8
  126.3 2.2 copy-start.7
  128.5 2.2 copy-start.2
  132.0 3.6 %copy-start.6 = (bf16[2,128,64,128]{3,2,1,0:T(8,128)(2,1)S(1)}, bf16[2,128,64,128]{3,2,1,0:T(8,128)(2,1)}, u32[]{:S(2)}) copy-start(bf16[2,128,64,128]{3,2,1,0:T(8,128)(2,1)} %get-tuple-element.5) | copy-start | bytes 12582916
  136.8 6.2 %copy-start.4 = (pred[128,64,256]{2,1,0:T(8,128)(4,1)S(1)}, pred[128,64,256]{2,1,0:T(8,128)(4,1)}, u32[]{:S(2)}) copy-start(pred[128,64,256]{2,1,0:T(8,128)(4,1)} %broadcast_and_fusion) | copy-start | bytes 6291460
  (1 other events, 1.3 us)
